TPU v7x, 128 devices: a whole 4x4x4 slice. The times are simulated.
128 devices in a mesh: dp: 8 (over z, y_lo), ctx: 16 (over y_hi, x, core).
Axes of the slice: x: 4, y: 4 (y_hi: 2, y_lo: 2; y = y_hi * 2 + y_lo), z: 4, core: 2. Of those that a mesh axis runs over, the one named last changes fastest.
Arguments:
- queries: bfloat16 [32768, 4096], P(('dp', 'ctx')), parts along dimension 0, may hold values from -5 to 5
- keys_values: bfloat16 [32768, 2, 1024], P(('dp', 'ctx')), parts along dimension 0, may hold values from -5 to 5
- fold: int32 [256], P('dp'), parts along dimension 0, may hold values from 0 to 31, each once
- doc_length: int32 [8], P('dp'), parts along dimension 0, may hold values from 2048 to 4096
Outputs:
- attended: bfloat16 [32768, 4096], P(('dp', 'ctx')), parts along dimension 0
There are 8 independent parts, one for each index of `dp`. A program takes and returns all parts, laid end to end along the dimension named above; each array names one. Nothing has to cross between parts.
Inputs may be any that keep to these rules, and one draw needn't show every extreme that they name: A permutation: slot s, the stored rows s * 128 to (s + 1) * 128 - 1, holds positions fold[s] * 128 onwards. `doc_length`: positions at or beyond it are padding.
All inputs are finite; a program needn't handle non-finite values.
Results may differ from a plain program's by a relative error of at most 0.004.
Values may be sent and summed in bfloat16 or wider, within the bound.
A program may use at most 320 MiB of HBM per device.

v0:
```python
import math

import jax
import jax.numpy as jnp
from jax import lax
from jax.sharding import PartitionSpec as P

HEADS = 32
KV_HEADS = 8
HEAD_DIM = 128


def from_behind(block, axis, distance):
    devices = range(lax.axis_size(axis))
    route = [((i - distance) % len(devices), i) for i in devices]
    return lax.ppermute(block, axis, route)


def shards(queries, keys_values, fold, doc_length):
    cycle_size = lax.axis_size("ctx")
    my_index = lax.axis_index("ctx")
    row_count = queries.shape[0]
    span_rows = row_count // 2
    group_size = HEADS // KV_HEADS
    score_scale = 1.0 / math.sqrt(HEAD_DIM)
    span_ids = jnp.arange(fold.shape[0], dtype=jnp.int32)
    length = doc_length[0]

    def positions(row_ids):
        slot_ids = row_ids // span_rows
        span_of = jnp.sum(
            jnp.where(slot_ids[:, None] == span_ids[None, :], fold[None, :], 0), axis=1
        )
        return span_of * span_rows + row_ids % span_rows

    query_pos = positions(my_index * row_count + jnp.arange(row_count, dtype=jnp.int32))
    query_block = queries.reshape(row_count, KV_HEADS, group_size, HEAD_DIM)

    def absorb(state_now, segment, offset_row):
        block_rows = segment.shape[0]
        key_pos = positions(offset_row + jnp.arange(block_rows, dtype=jnp.int32))
        visible = (key_pos[None, :] <= query_pos[:, None]) & (key_pos < length)[None, :]
        running_max, weight_sum, numerator = state_now
        key_block = segment[:, 0].reshape(block_rows, KV_HEADS, HEAD_DIM)
        value_block = segment[:, 1].reshape(block_rows, KV_HEADS, HEAD_DIM)
        scores = (
            jnp.einsum("qgjd,kgd->qgjk", query_block, key_block, preferred_element_type=jnp.float32)
            * score_scale
        )
        key_mask = visible[:, None, None, :]
        scores = jnp.where(key_mask, scores, -1e30)
        new_max = jnp.maximum(running_max, jnp.max(scores, axis=3))
        weights = jnp.where(key_mask, jnp.exp(scores - new_max[..., None]), 0.0)
        rescale = jnp.exp(running_max - new_max)
        weight_sum = weight_sum * rescale + jnp.sum(weights, axis=3)
        product = jnp.einsum(
            "qgjk,kgd->qgjd",
            weights.astype(jnp.bfloat16),
            value_block,
            preferred_element_type=jnp.float32,
        )
        numerator = numerator * rescale[..., None] + product
        return (new_max, weight_sum, numerator)

    initial = (
        jnp.full((row_count, KV_HEADS, group_size), -1e30, jnp.float32),
        jnp.zeros((row_count, KV_HEADS, group_size), jnp.float32),
        jnp.zeros((row_count, KV_HEADS, group_size, HEAD_DIM), jnp.float32),
    )
    state_now = absorb(initial, keys_values, my_index * row_count)

    def turn(turn_index, carried):
        state_in, travelling = carried
        travelling = from_behind(travelling, "ctx", 1)
        anchor = (my_index - turn_index) % cycle_size
        return (absorb(state_in, travelling, anchor * row_count), travelling)

    state_now, _ = lax.fori_loop(1, cycle_size, turn, (state_now, keys_values))
    _, weight_sum, numerator = state_now
    result = (numerator / weight_sum[..., None]).reshape(row_count, HEADS * HEAD_DIM)
    result = jnp.where((query_pos < length)[:, None], result, 0.0)
    return result.astype(jnp.bfloat16)


def solution(mesh):
    in_specs = (P(("dp", "ctx"), None), P(("dp", "ctx"), None, None), P("dp"), P("dp"))
    out_specs = P(("dp", "ctx"), None)
    return jax.shard_map(shards, mesh=mesh, in_specs=in_specs, out_specs=out_specs, check_vma=False)
```

profile of v0, /device:TPU:80, one launch (start us, length us, event | category | flops | bytes accessed | tf_op | source)
XLA Modules:
  0.0 452.9 jit_solution(8880169277256179238)
XLA Ops:
  4.9 4.1 copy.25
  17.4 4.7 %bitcast_add_fusion.1 = f32[256,8,4,128]{3,0,2,1:T(8,128)} fusion(f32[256,8,4]{0,2,1:T(4,128)S(1)} %get-tuple-element.386, bf16[256,8,128,1]{0,2,3,1:T(8,128)(2,1)S(1)} %bitcast.106, f32[8,256,256,4]{2,1,3,0:T(8,128)S(1)} %get-tuple-element.389, f32[256,8,4]{0,2,1:T(4,128)S(1)} %broadcast_maximum_fusion, pred[256,256]{0,1:T(8,128)(4,1)S(1)} %compare_and_fusion.1), kind=kOutput, calls=%fused_computation.37 | convolution fusion | flops 548405248 | bytes 13238272 | tf_op jit(solution)/shard_map/qgjk,kgd->qgjd/dot_general | solution.py:56
  22.1 419.6 %while.23 = (s32[]{:T(128)}, f32[256,8,4]{0,2,1:T(4,128)S(1)}, f32[256,8,4]{0,2,1:T(4,128)S(1)}, f32[256,8,4,128]{3,0,2,1:T(8,128)}, bf16[256,2,1024]{0,2,1:T(8,...) while((s32[]{:T(128)}, f32[256,8,4]{0,2,1:T(4,128)S(1)}, ...), condition=%wide.region_7.8_spmd.clone, body=%wide.region_3.7_spmd.clone.sunk | while | flops 1103281664 | bytes 79437816 | solution.py:78
  23.0 17.1 %collective-permute-done = bf16[256,2,1024]{0,2,1:T(8,128)(2,1)S(1)} collective-permute-done((bf16[256,2,1024]{0,2,1:T(8,128)(2,1)}, bf16[256,2,1024]{0,2,1:T(8,128)(2,1)S(1)}, u32[]{:S(2)}, u32[]{:S(2)}) %collective-permute-start) | collective-permute-done | bytes 1048608 | tf_op jit(solution)/shard_map/while/body/eval_jaxpr/ppermute | solution.py:16
  44.0 3.8 bitcast_add_fusion.3
  51.0 17.1 %collective-permute-done = bf16[256,2,1024]{0,2,1:T(8,128)(2,1)S(1)} collective-permute-done((bf16[256,2,1024]{0,2,1:T(8,128)(2,1)}, bf16[256,2,1024]{0,2,1:T(8,128)(2,1)S(1)}, u32[]{:S(2)}, u32[]{:S(2)}) %collective-permute-start) | collective-permute-done | bytes 1048608 | tf_op jit(solution)/shard_map/while/body/eval_jaxpr/ppermute | solution.py:16
  72.0 3.8 bitcast_add_fusion.3
  79.0 17.1 %collective-permute-done = bf16[256,2,1024]{0,2,1:T(8,128)(2,1)S(1)} collective-permute-done((bf16[256,2,1024]{0,2,1:T(8,128)(2,1)}, bf16[256,2,1024]{0,2,1:T(8,128)(2,1)S(1)}, u32[]{:S(2)}, u32[]{:S(2)}) %collective-permute-start) | collective-permute-done | bytes 1048608 | tf_op jit(solution)/shard_map/while/body/eval_jaxpr/ppermute | solution.py:16
  100.0 3.8 bitcast_add_fusion.3
  107.0 17.1 %collective-permute-done = bf16[256,2,1024]{0,2,1:T(8,128)(2,1)S(1)} collective-permute-done((bf16[256,2,1024]{0,2,1:T(8,128)(2,1)}, bf16[256,2,1024]{0,2,1:T(8,128)(2,1)S(1)}, u32[]{:S(2)}, u32[]{:S(2)}) %collective-permute-start) | collective-permute-done | bytes 1048608 | tf_op jit(solution)/shard_map/while/body/eval_jaxpr/ppermute | solution.py:16
  134.9 17.1 %collective-permute-done = bf16[256,2,1024]{0,2,1:T(8,128)(2,1)S(1)} collective-permute-done((bf16[256,2,1024]{0,2,1:T(8,128)(2,1)}, bf16[256,2,1024]{0,2,1:T(8,128)(2,1)S(1)}, u32[]{:S(2)}, u32[]{:S(2)}) %collective-permute-start) | collective-permute-done | bytes 1048608 | tf_op jit(solution)/shard_map/while/body/eval_jaxpr/ppermute | solution.py:16
  162.9 17.1 %collective-permute-done = bf16[256,2,1024]{0,2,1:T(8,128)(2,1)S(1)} collective-permute-done((bf16[256,2,1024]{0,2,1:T(8,128)(2,1)}, bf16[256,2,1024]{0,2,1:T(8,128)(2,1)S(1)}, u32[]{:S(2)}, u32[]{:S(2)}) %collective-permute-start) | collective-permute-done | bytes 1048608 | tf_op jit(solution)/shard_map/while/body/eval_jaxpr/ppermute | solution.py:16
  183.9 3.8 bitcast_add_fusion.3
  190.9 17.1 %collective-permute-done = bf16[256,2,1024]{0,2,1:T(8,128)(2,1)S(1)} collective-permute-done((bf16[256,2,1024]{0,2,1:T(8,128)(2,1)}, bf16[256,2,1024]{0,2,1:T(8,128)(2,1)S(1)}, u32[]{:S(2)}, u32[]{:S(2)}) %collective-permute-start) | collective-permute-done | bytes 1048608 | tf_op jit(solution)/shard_map/while/body/eval_jaxpr/ppermute | solution.py:16
  211.9 3.8 bitcast_add_fusion.3
  218.9 17.1 %collective-permute-done = bf16[256,2,1024]{0,2,1:T(8,128)(2,1)S(1)} collective-permute-done((bf16[256,2,1024]{0,2,1:T(8,128)(2,1)}, bf16[256,2,1024]{0,2,1:T(8,128)(2,1)S(1)}, u32[]{:S(2)}, u32[]{:S(2)}) %collective-permute-start) | collective-permute-done | bytes 1048608 | tf_op jit(solution)/shard_map/while/body/eval_jaxpr/ppermute | solution.py:16
  239.9 3.8 bitcast_add_fusion.3
  246.8 17.1 %collective-permute-done = bf16[256,2,1024]{0,2,1:T(8,128)(2,1)S(1)} collective-permute-done((bf16[256,2,1024]{0,2,1:T(8,128)(2,1)}, bf16[256,2,1024]{0,2,1:T(8,128)(2,1)S(1)}, u32[]{:S(2)}, u32[]{:S(2)}) %collective-permute-start) | collective-permute-done | bytes 1048608 | tf_op jit(solution)/shard_map/while/body/eval_jaxpr/ppermute | solution.py:16
  274.8 17.1 %collective-permute-done = bf16[256,2,1024]{0,2,1:T(8,128)(2,1)S(1)} collective-permute-done((bf16[256,2,1024]{0,2,1:T(8,128)(2,1)}, bf16[256,2,1024]{0,2,1:T(8,128)(2,1)S(1)}, u32[]{:S(2)}, u32[]{:S(2)}) %collective-permute-start) | collective-permute-done | bytes 1048608 | tf_op jit(solution)/shard_map/while/body/eval_jaxpr/ppermute | solution.py:16
  302.8 17.1 %collective-permute-done = bf16[256,2,1024]{0,2,1:T(8,128)(2,1)S(1)} collective-permute-done((bf16[256,2,1024]{0,2,1:T(8,128)(2,1)}, bf16[256,2,1024]{0,2,1:T(8,128)(2,1)S(1)}, u32[]{:S(2)}, u32[]{:S(2)}) %collective-permute-start) | collective-permute-done | bytes 1048608 | tf_op jit(solution)/shard_map/while/body/eval_jaxpr/ppermute | solution.py:16
  330.8 17.1 %collective-permute-done = bf16[256,2,1024]{0,2,1:T(8,128)(2,1)S(1)} collective-permute-done((bf16[256,2,1024]{0,2,1:T(8,128)(2,1)}, bf16[256,2,1024]{0,2,1:T(8,128)(2,1)S(1)}, u32[]{:S(2)}, u32[]{:S(2)}) %collective-permute-start) | collective-permute-done | bytes 1048608 | tf_op jit(solution)/shard_map/while/body/eval_jaxpr/ppermute | solution.py:16
  358.7 17.1 %collective-permute-done = bf16[256,2,1024]{0,2,1:T(8,128)(2,1)S(1)} collective-permute-done((bf16[256,2,1024]{0,2,1:T(8,128)(2,1)}, bf16[256,2,1024]{0,2,1:T(8,128)(2,1)S(1)}, u32[]{:S(2)}, u32[]{:S(2)}) %collective-permute-start) | collective-permute-done | bytes 1048608 | tf_op jit(solution)/shard_map/while/body/eval_jaxpr/ppermute | solution.py:16
  386.7 17.1 %collective-permute-done = bf16[256,2,1024]{0,2,1:T(8,128)(2,1)S(1)} collective-permute-done((bf16[256,2,1024]{0,2,1:T(8,128)(2,1)}, bf16[256,2,1024]{0,2,1:T(8,128)(2,1)S(1)}, u32[]{:S(2)}, u32[]{:S(2)}) %collective-permute-start) | collective-permute-done | bytes 1048608 | tf_op jit(solution)/shard_map/while/body/eval_jaxpr/ppermute | solution.py:16
  414.7 17.1 %collective-permute-done = bf16[256,2,1024]{0,2,1:T(8,128)(2,1)S(1)} collective-permute-done((bf16[256,2,1024]{0,2,1:T(8,128)(2,1)}, bf16[256,2,1024]{0,2,1:T(8,128)(2,1)S(1)}, u32[]{:S(2)}, u32[]{:S(2)}) %collective-permute-start) | collective-permute-done | bytes 1048608 | tf_op jit(solution)/shard_map/while/body/eval_jaxpr/ppermute | solution.py:16
  (270 shorter events, 162.3 us)
Async XLA Ops:
  4.0 5.0 %copy-start.2 = (bf16[256,2,1024]{0,2,1:T(8,128)(2,1)}, bf16[256,2,1024]{0,2,1:T(8,128)(2,1)S(1)}, u32[]{:S(2)}) copy-start(bf16[256,2,1024]{0,2,1:T(8,128)(2,1)S(1)} %copy.24) | copy-start | bytes 3145732
  12.0 5.4 %copy-start.3 = (bf16[256,1,1024]{0,2,1:T(8,128)(2,1)S(1)}, bf16[256,1,1024]{0,2,1:T(8,128)(2,1)}, u32[]{:S(2)}) copy-start(bf16[256,1,1024]{0,2,1:T(8,128)(2,1)} %get-tuple-element.384) | copy-start | bytes 1572868
  17.4 4.7 %copy-start.4 = (s32[32]{0:T(128)S(1)}, s32[32]{0:T(128)}, u32[]{:S(2)}) copy-start(s32[32]{0:T(128)} %param.8) | copy-start | bytes 388
  22.1 18.0 %collective-permute-start = (bf16[256,2,1024]{0,2,1:T(8,128)(2,1)}, bf16[256,2,1024]{0,2,1:T(8,128)(2,1)S(1)}, u32[]{:S(2)}, u32[]{:S(2)}) collective-permute-start(bf16[256,2,1024]{0,2,1:T(8,128)(2,1)} %get-tuple-element.490), channel_id=1, source_target_pairs={{15,0},{0,1},{1,2},{2,3},{3,4},{4,5},{5,6},{6,7},{7,8},{8,9},{9,10... | collective-permute-start | bytes 3145736 | tf_op jit(solution)/shard_map/while/body/eval_jaxpr/ppermute | solution.py:16
  50.1 18.0 %collective-permute-start = (bf16[256,2,1024]{0,2,1:T(8,128)(2,1)}, bf16[256,2,1024]{0,2,1:T(8,128)(2,1)S(1)}, u32[]{:S(2)}, u32[]{:S(2)}) collective-permute-start(bf16[256,2,1024]{0,2,1:T(8,128)(2,1)} %get-tuple-element.490), channel_id=1, source_target_pairs={{15,0},{0,1},{1,2},{2,3},{3,4},{4,5},{5,6},{6,7},{7,8},{8,9},{9,10... | collective-permute-start | bytes 3145736 | tf_op jit(solution)/shard_map/while/body/eval_jaxpr/ppermute | solution.py:16
  78.1 18.0 %collective-permute-start = (bf16[256,2,1024]{0,2,1:T(8,128)(2,1)}, bf16[256,2,1024]{0,2,1:T(8,128)(2,1)S(1)}, u32[]{:S(2)}, u32[]{:S(2)}) collective-permute-start(bf16[256,2,1024]{0,2,1:T(8,128)(2,1)} %get-tuple-element.490), channel_id=1, source_target_pairs={{15,0},{0,1},{1,2},{2,3},{3,4},{4,5},{5,6},{6,7},{7,8},{8,9},{9,10... | collective-permute-start | bytes 3145736 | tf_op jit(solution)/shard_map/while/body/eval_jaxpr/ppermute | solution.py:16
  96.2 3.8 copy-start
  106.0 18.0 %collective-permute-start = (bf16[256,2,1024]{0,2,1:T(8,128)(2,1)}, bf16[256,2,1024]{0,2,1:T(8,128)(2,1)S(1)}, u32[]{:S(2)}, u32[]{:S(2)}) collective-permute-start(bf16[256,2,1024]{0,2,1:T(8,128)(2,1)} %get-tuple-element.490), channel_id=1, source_target_pairs={{15,0},{0,1},{1,2},{2,3},{3,4},{4,5},{5,6},{6,7},{7,8},{8,9},{9,10... | collective-permute-start | bytes 3145736 | tf_op jit(solution)/shard_map/while/body/eval_jaxpr/ppermute | solution.py:16
  124.2 3.8 copy-start
  134.0 18.0 %collective-permute-start = (bf16[256,2,1024]{0,2,1:T(8,128)(2,1)}, bf16[256,2,1024]{0,2,1:T(8,128)(2,1)S(1)}, u32[]{:S(2)}, u32[]{:S(2)}) collective-permute-start(bf16[256,2,1024]{0,2,1:T(8,128)(2,1)} %get-tuple-element.490), channel_id=1, source_target_pairs={{15,0},{0,1},{1,2},{2,3},{3,4},{4,5},{5,6},{6,7},{7,8},{8,9},{9,10... | collective-permute-start | bytes 3145736 | tf_op jit(solution)/shard_map/while/body/eval_jaxpr/ppermute | solution.py:16
  152.1 3.8 copy-start
  162.0 18.0 %collective-permute-start = (bf16[256,2,1024]{0,2,1:T(8,128)(2,1)}, bf16[256,2,1024]{0,2,1:T(8,128)(2,1)S(1)}, u32[]{:S(2)}, u32[]{:S(2)}) collective-permute-start(bf16[256,2,1024]{0,2,1:T(8,128)(2,1)} %get-tuple-element.490), channel_id=1, source_target_pairs={{15,0},{0,1},{1,2},{2,3},{3,4},{4,5},{5,6},{6,7},{7,8},{8,9},{9,10... | collective-permute-start | bytes 3145736 | tf_op jit(solution)/shard_map/while/body/eval_jaxpr/ppermute | solution.py:16
  180.1 3.8 copy-start
  190.0 18.0 %collective-permute-start = (bf16[256,2,1024]{0,2,1:T(8,128)(2,1)}, bf16[256,2,1024]{0,2,1:T(8,128)(2,1)S(1)}, u32[]{:S(2)}, u32[]{:S(2)}) collective-permute-start(bf16[256,2,1024]{0,2,1:T(8,128)(2,1)} %get-tuple-element.490), channel_id=1, source_target_pairs={{15,0},{0,1},{1,2},{2,3},{3,4},{4,5},{5,6},{6,7},{7,8},{8,9},{9,10... | collective-permute-start | bytes 3145736 | tf_op jit(solution)/shard_map/while/body/eval_jaxpr/ppermute | solution.py:16
  208.1 3.8 copy-start
  217.9 18.0 %collective-permute-start = (bf16[256,2,1024]{0,2,1:T(8,128)(2,1)}, bf16[256,2,1024]{0,2,1:T(8,128)(2,1)S(1)}, u32[]{:S(2)}, u32[]{:S(2)}) collective-permute-start(bf16[256,2,1024]{0,2,1:T(8,128)(2,1)} %get-tuple-element.490), channel_id=1, source_target_pairs={{15,0},{0,1},{1,2},{2,3},{3,4},{4,5},{5,6},{6,7},{7,8},{8,9},{9,10... | collective-permute-start | bytes 3145736 | tf_op jit(solution)/shard_map/while/body/eval_jaxpr/ppermute | solution.py:16
  245.9 18.0 %collective-permute-start = (bf16[256,2,1024]{0,2,1:T(8,128)(2,1)}, bf16[256,2,1024]{0,2,1:T(8,128)(2,1)S(1)}, u32[]{:S(2)}, u32[]{:S(2)}) collective-permute-start(bf16[256,2,1024]{0,2,1:T(8,128)(2,1)} %get-tuple-element.490), channel_id=1, source_target_pairs={{15,0},{0,1},{1,2},{2,3},{3,4},{4,5},{5,6},{6,7},{7,8},{8,9},{9,10... | collective-permute-start | bytes 3145736 | tf_op jit(solution)/shard_map/while/body/eval_jaxpr/ppermute | solution.py:16
  273.9 18.0 %collective-permute-start = (bf16[256,2,1024]{0,2,1:T(8,128)(2,1)}, bf16[256,2,1024]{0,2,1:T(8,128)(2,1)S(1)}, u32[]{:S(2)}, u32[]{:S(2)}) collective-permute-start(bf16[256,2,1024]{0,2,1:T(8,128)(2,1)} %get-tuple-element.490), channel_id=1, source_target_pairs={{15,0},{0,1},{1,2},{2,3},{3,4},{4,5},{5,6},{6,7},{7,8},{8,9},{9,10... | collective-permute-start | bytes 3145736 | tf_op jit(solution)/shard_map/while/body/eval_jaxpr/ppermute | solution.py:16
  292.0 3.8 copy-start
  301.9 18.0 %collective-permute-start = (bf16[256,2,1024]{0,2,1:T(8,128)(2,1)}, bf16[256,2,1024]{0,2,1:T(8,128)(2,1)S(1)}, u32[]{:S(2)}, u32[]{:S(2)}) collective-permute-start(bf16[256,2,1024]{0,2,1:T(8,128)(2,1)} %get-tuple-element.490), channel_id=1, source_target_pairs={{15,0},{0,1},{1,2},{2,3},{3,4},{4,5},{5,6},{6,7},{7,8},{8,9},{9,10... | collective-permute-start | bytes 3145736 | tf_op jit(solution)/shard_map/while/body/eval_jaxpr/ppermute | solution.py:16
  329.8 18.0 %collective-permute-start = (bf16[256,2,1024]{0,2,1:T(8,128)(2,1)}, bf16[256,2,1024]{0,2,1:T(8,128)(2,1)S(1)}, u32[]{:S(2)}, u32[]{:S(2)}) collective-permute-start(bf16[256,2,1024]{0,2,1:T(8,128)(2,1)} %get-tuple-element.490), channel_id=1, source_target_pairs={{15,0},{0,1},{1,2},{2,3},{3,4},{4,5},{5,6},{6,7},{7,8},{8,9},{9,10... | collective-permute-start | bytes 3145736 | tf_op jit(solution)/shard_map/while/body/eval_jaxpr/ppermute | solution.py:16
  357.8 18.0 %collective-permute-start = (bf16[256,2,1024]{0,2,1:T(8,128)(2,1)}, bf16[256,2,1024]{0,2,1:T(8,128)(2,1)S(1)}, u32[]{:S(2)}, u32[]{:S(2)}) collective-permute-start(bf16[256,2,1024]{0,2,1:T(8,128)(2,1)} %get-tuple-element.490), channel_id=1, source_target_pairs={{15,0},{0,1},{1,2},{2,3},{3,4},{4,5},{5,6},{6,7},{7,8},{8,9},{9,10... | collective-permute-start | bytes 3145736 | tf_op jit(solution)/shard_map/while/body/eval_jaxpr/ppermute | solution.py:16
  385.8 18.0 %collective-permute-start = (bf16[256,2,1024]{0,2,1:T(8,128)(2,1)}, bf16[256,2,1024]{0,2,1:T(8,128)(2,1)S(1)}, u32[]{:S(2)}, u32[]{:S(2)}) collective-permute-start(bf16[256,2,1024]{0,2,1:T(8,128)(2,1)} %get-tuple-element.490), channel_id=1, source_target_pairs={{15,0},{0,1},{1,2},{2,3},{3,4},{4,5},{5,6},{6,7},{7,8},{8,9},{9,10... | collective-permute-start | bytes 3145736 | tf_op jit(solution)/shard_map/while/body/eval_jaxpr/ppermute | solution.py:16
  413.8 18.0 %collective-permute-start = (bf16[256,2,1024]{0,2,1:T(8,128)(2,1)}, bf16[256,2,1024]{0,2,1:T(8,128)(2,1)S(1)}, u32[]{:S(2)}, u32[]{:S(2)}) collective-permute-start(bf16[256,2,1024]{0,2,1:T(8,128)(2,1)} %get-tuple-element.490), channel_id=1, source_target_pairs={{15,0},{0,1},{1,2},{2,3},{3,4},{4,5},{5,6},{6,7},{7,8},{8,9},{9,10... | collective-permute-start | bytes 3145736 | tf_op jit(solution)/shard_map/while/body/eval_jaxpr/ppermute | solution.py:16
  (24 other events, 67.7 us)
where the time goes:
time: 453 us
  waiting for transfers between devices  257 us (57%)
  matrix products  88.2 us (19%)
  other arithmetic  54.3 us (12%)
  local copies, waits for them, and re-layouts  51.3 us (11%)
    ppermute x15, waiting for transfers between devices, from_behind(): return lax.ppermute(block, axis, route)  257 us
    dot_general x16, matrix products, absorb(): jnp.einsum('qgjk,kgd->qgjd', weights.astype(jnp.bfloat16), value_block, p...  61.8 us
    reduce_sum x16, other arithmetic, absorb(): weight_sum = weight_sum * rescale + jnp.sum(weights, axis=3)  34.5 us
    while x90, local copies, waits for them, and re-layouts  33.6 us
    dot_general x16, matrix products, absorb(): jnp.einsum('qgjd,kgd->qgjk', query_block, key_block, preferred_element_ty...  26.4 us
    lt x15, other arithmetic, absorb(): key_pos < length  9.88 us
    unnamed x9, local copies, waits for them, and re-layouts  9.53 us
  transfers between devices with their start and end apart: 15, of which 15 were waited for; matrix products, arithmetic and copies ran while one was open for 3% of the time, Pallas kernels for 0%

commit v1 on v0

v1 whole, which is shorter than its diff:
```python
import functools
import math

import jax
import jax.numpy as jnp
from jax import lax
from jax.experimental import pallas as pl
from jax.experimental.pallas import tpu as pltpu
from jax.sharding import PartitionSpec as P

HEADS = 32
KV_HEADS = 8
GROUP = 4
DIM = 128
SPAN = 128
EXP_SCALE = math.log2(math.e) / math.sqrt(DIM)
HIDDEN = -1e30
LIMIT = 2.0**110
CHUNKS = 4
TILE_BLOCKS = 4
NT = (((1,), (1,)), ((), ()))


def scores_t(keys, queries):
    return lax.dot_general(keys, queries, NT, preferred_element_type=jnp.float32)


def weights_of(scores):
    return jnp.exp2(scores * EXP_SCALE).astype(jnp.bfloat16)


def with_ones(values_t):
    ones = jnp.ones((16, values_t.shape[1]), jnp.bfloat16)
    return jnp.concatenate([values_t, ones], axis=0)


def attend(me_ref, q_ref, kv_ref, hide_ref, live_ref, o_ref, slot_ref, qx_ref, *acc_refs):
    me = me_ref[0]
    blocks, rows = kv_ref.shape[0], kv_ref.shape[3]
    spans = rows // SPAN
    tile_rows = TILE_BLOCKS * rows

    row = lax.broadcasted_iota(jnp.int32, (SPAN, SPAN), 0)
    lane = lax.broadcasted_iota(jnp.int32, (SPAN, SPAN), 1)

    @pl.when(pl.program_id(0) == 0)
    def _():
        for t in range(blocks * spans):
            slot_ref[t] = jnp.where((lane == 0) | (lane == 1 + t), 1.0, 0.0).astype(jnp.bfloat16)

    def keys_of(b):
        return kv_ref[b, 0, 0]

    def values_of(b):
        return [kv_ref[b, 1, 0, t * SPAN : (t + 1) * SPAN] for t in range(spans)]

    def slots_of(b):
        return [slot_ref[b * spans + t] for t in range(spans)]

    own_keys = keys_of(me)
    own_values = values_of(me)
    for i in range(GROUP):
        for t in range(spans):
            cut = slice(t * SPAN, (t + 1) * SPAN)
            q = q_ref[cut, i * DIM : (i + 1) * DIM]
            keys = own_keys[cut]
            near = jnp.where(lane <= row, scores_t(q, keys), HIDDEN)
            best = jnp.max(near, axis=1, keepdims=True).astype(jnp.bfloat16)
            extra = jnp.where(lane == 0, -best.astype(jnp.float32), hide_ref[cut].astype(jnp.float32))
            qx_ref[i, cut, :DIM] = q
            qx_ref[i, cut, DIM:] = extra.astype(jnp.bfloat16)
            first = jnp.where(lane == 0, 1.0, 0.0).astype(jnp.bfloat16)
            keys_x = jnp.concatenate([keys, first], axis=1)
            shifted = scores_t(keys_x, qx_ref[i, cut])
            weights = weights_of(jnp.where(row <= lane, shifted, HIDDEN))
            acc_refs[i][:, cut] = jnp.dot(
                with_ones(own_values[t]), weights, preferred_element_type=jnp.float32
            )

    @pl.loop(0, blocks // TILE_BLOCKS)
    def _(tile):
        first = tile * TILE_BLOCKS
        keys = jnp.concatenate([keys_of(first + b) for b in range(TILE_BLOCKS)], axis=0)
        slots = jnp.concatenate(
            [s for b in range(TILE_BLOCKS) for s in slots_of(first + b)], axis=0
        )
        keys_x = jnp.concatenate([keys, slots], axis=1)
        values_t = with_ones(
            jnp.concatenate([v for b in range(TILE_BLOCKS) for v in values_of(first + b)], axis=1)
        )

        def add(i, weights):
            acc_refs[i][...] += jnp.dot(values_t, weights, preferred_element_type=jnp.float32)

        held = None
        for i in range(GROUP):
            weights = weights_of(scores_t(keys_x, qx_ref[i]))
            if held is not None:
                add(i - 1, held)
            held = weights
        add(GROUP - 1, held)

    live = live_ref[0:1]

    def finish(i):
        acc = acc_refs[i][...]
        out = jnp.where(live > 0.0, acc[:DIM] / acc[DIM : DIM + 1], 0.0)
        o_ref[:, i * DIM : (i + 1) * DIM] = out.T.astype(jnp.bfloat16)

    top = acc_refs[0][DIM : DIM + 1]
    for i in range(1, GROUP):
        top = jnp.where(acc_refs[i][DIM : DIM + 1] < LIMIT, top, jnp.inf)
    good = jnp.min(jnp.where(top < LIMIT, 1.0, 0.0)) > 0.0

    for i in range(GROUP):
        finish(i)

    @pl.when(jnp.logical_not(good))
    def _():
        for i in range(GROUP):
            parts = []
            for t in range(spans):
                cut = slice(t * SPAN, (t + 1) * SPAN)
                near = scores_t(own_keys[cut], q_ref[cut, i * DIM : (i + 1) * DIM])
                near = jnp.where(row <= lane, near, HIDDEN)
                best = jnp.max(near, axis=0, keepdims=True)
                acc_refs[i][:, cut] = jnp.dot(
                    with_ones(own_values[t]), weights_of(near - best), preferred_element_type=jnp.float32
                )
                qx_ref[i, cut, DIM:] = jnp.where(
                    lane == 0, 0.0, hide_ref[cut].astype(jnp.float32)
                ).astype(jnp.bfloat16)
                parts.append(best)

            def absorb(b, best):
                keys_x = jnp.concatenate([keys_of(b), jnp.concatenate(slots_of(b), axis=0)], axis=1)
                scores = scores_t(keys_x, qx_ref[i])
                new = jnp.maximum(best, jnp.max(scores, axis=0, keepdims=True))
                values_t = with_ones(jnp.concatenate(values_of(b), axis=1))
                acc_refs[i][...] = acc_refs[i][...] * jnp.exp2((best - new) * EXP_SCALE) + jnp.dot(
                    values_t, weights_of(scores - new), preferred_element_type=jnp.float32
                )
                return new

            lax.fori_loop(0, blocks, absorb, jnp.concatenate(parts, axis=1))
            finish(i)


def shards(queries, keys_values, fold, doc_length):
    size = lax.axis_size("ctx")
    me = lax.axis_index("ctx")
    rows = queries.shape[0]
    spans = rows // SPAN
    slots = fold.shape[0]

    split = keys_values.reshape(rows, 2, KV_HEADS, DIM)
    keys = split[:, 0].transpose(1, 0, 2)
    values = split[:, 1].reshape(spans, SPAN, KV_HEADS, DIM).transpose(2, 0, 3, 1)
    packed = jnp.stack([keys, values.reshape(KV_HEADS, rows, DIM)])

    own = lax.dynamic_slice(fold, (me * spans,), (spans,))
    own_span = jnp.repeat(own, SPAN)
    hidden = fold[None, :] >= own_span[:, None]
    hide = jnp.where(hidden, HIDDEN, 0.0).astype(jnp.bfloat16)
    hide = jnp.pad(hide, ((0, 0), (1, DIM - 1 - slots)))
    position = own_span * SPAN + jnp.arange(rows, dtype=jnp.int32) % SPAN
    live = jnp.where(position < doc_length[0], 1.0, 0.0)
    live = jnp.broadcast_to(live[None, :], (8, rows))

    heads = KV_HEADS // CHUNKS
    call = pl.pallas_call(
        attend,
        grid_spec=pltpu.PrefetchScalarGridSpec(
            num_scalar_prefetch=1,
            grid=(heads,),
            in_specs=[
                pl.BlockSpec((rows, GROUP * DIM), lambda g, s: (0, s[1] * heads + g)),
                pl.BlockSpec((size, 2, 1, rows, DIM), lambda g, s: (0, 0, g, 0, 0)),
                pl.BlockSpec((rows, DIM), lambda g, s: (0, 0)),
                pl.BlockSpec((8, rows), lambda g, s: (0, 0)),
            ],
            out_specs=pl.BlockSpec((rows, GROUP * DIM), lambda g, s: (0, g)),
            scratch_shapes=[
                pltpu.VMEM((slots, SPAN, DIM), jnp.bfloat16),
                pltpu.VMEM((GROUP, rows, 2 * DIM), jnp.bfloat16),
            ]
            + [pltpu.VMEM((DIM + 16, rows), jnp.float32)] * GROUP,
        ),
        out_shape=jax.ShapeDtypeStruct((rows, heads * GROUP * DIM), jnp.bfloat16),
        compiler_params=pltpu.CompilerParams(vmem_limit_bytes=40 * 2**20),
        cost_estimate=pl.CostEstimate(
            flops=4 * rows * size * rows * heads * GROUP * DIM,
            transcendentals=rows * size * rows * heads * GROUP,
            bytes_accessed=size * 4 * heads * rows * DIM,
        ),
    )
    outs = []
    for c in range(CHUNKS):
        whole = lax.all_gather(packed[:, c * heads : (c + 1) * heads], "ctx")
        outs.append(call(jnp.stack([me, c]), queries, whole, hide, live))
    return jnp.concatenate(outs, axis=1)


def solution(mesh):
    in_specs = (P(("dp", "ctx"), None), P(("dp", "ctx"), None, None), P("dp"), P("dp"))
    out_specs = P(("dp", "ctx"), None)
    return jax.shard_map(shards, mesh=mesh, in_specs=in_specs, out_specs=out_specs, check_vma=False)
```

time: 453 us -> 273 us (0.60)
  the two profiles are of different devices: /device:TPU:80 before, /device:TPU:1 now
where the time goes in v1:
time: 273 us; the launch traced here: 272 us
  waiting for transfers between devices  169 us (62%)
  Pallas kernels  63.8 us (23%)
  local copies, waits for them, and re-layouts  23.8 us (9%)
  between operations  13.9 us (5%)
    all_gather x4, waiting for transfers between devices, shards(): whole = lax.all_gather(packed[:, c * heads:(c + 1) * heads], 'ctx')  169 us
    pallas_call x4, Pallas kernels, shards(): outs.append(call(jnp.stack([me, c]), queries, whole, hide, live))  63.8 us
    unnamed x19, local copies, waits for them, and re-layouts  17.5 us
  transfers between devices with their start and end apart: 4, of which 4 were waited for; matrix products, arithmetic and copies ran while one was open for 1% of the time, Pallas kernels for 18%

profile of v1, /device:TPU:1, one launch (start us, length us, event | category | flops | bytes accessed | tf_op | source)
XLA Modules:
  0.0 272.4 jit_solution(10393466786577169951)
XLA Ops:
  6.5 2.4 copy.8
  9.2 2.1 copy.9
  11.3 0.3 stack_reshape.3
  11.7 0.8 copy.10
  12.6 0.8 copy.11
  13.6 0.8 copy.13
  14.5 0.9 copy.12
  16.6 55.9 %all-gather.9.cloned.1.call-done = bf16[32,2,256,128]{3,2,1,0:T(8,128)(2,1)} async-done(((bf16[2,2,256,128]{3,2,1,0:T(8,128)(2,1)}), bf16[32,2,256,128]{3,2,1,0:T(8,128)(2,1)}) %all-gather.9.cloned.1.call-update) | async-done | bytes 4194320 | tf_op jit(solution)/shard_map/all_gather | solution.py:199
  72.5 2.2 copy-done
  74.7 1.6 copy-done.4
  76.3 15.9 %shard_map.46 = bf16[256,1024]{1,0:T(8,128)(2,1)S(1)} custom-call(s32[2]{0:T(128)S(1)} %get-tuple-element.11.me_ref, bf16[256,4096]{1,0:T(8,128)(2,1)S(1)} %copy-done.4, bf16[16,2,2,256,128]{4,3,2,1,0:T(8,128)(2,1)S(1)} %bitcast.24, bf16[256,128]{1,0:T(8,128)(2,1)S(1)} %pad.4.hide_ref, f32[8,256]{1,0:T(8,128)S(1)} %broadcast_in_dim.31.live_ref), custom_call_target="tpu_custom_call" | custom-call | flops 4294967296 | bytes 4194304 | tf_op jit(solution)/shard_map/pallas_call | solution.py:200
  92.2 37.7 %all-gather.11.cloned.1.call-done = bf16[32,2,256,128]{3,2,1,0:T(8,128)(2,1)} async-done(((bf16[2,2,256,128]{3,2,1,0:T(8,128)(2,1)}), bf16[32,2,256,128]{3,2,1,0:T(8,128)(2,1)}) %all-gather.11.cloned.1.call-update) | async-done | bytes 4194320 | tf_op jit(solution)/shard_map/all_gather | solution.py:199
  129.9 2.2 copy-done.1
  132.1 1.6 copy-done.5
  133.7 15.9 %shard_map.47 = bf16[256,1024]{1,0:T(8,128)(2,1)S(1)} custom-call(s32[2]{0:T(128)S(1)} %get-tuple-element.12.me_ref, bf16[256,4096]{1,0:T(8,128)(2,1)S(1)} %copy-done.5, bf16[16,2,2,256,128]{4,3,2,1,0:T(8,128)(2,1)S(1)} %bitcast.25, bf16[256,128]{1,0:T(8,128)(2,1)S(1)} %pad.4.hide_ref, f32[8,256]{1,0:T(8,128)S(1)} %broadcast_in_dim.31.live_ref), custom_call_target="tpu_custom_call" | custom-call | flops 4294967296 | bytes 4194304 | tf_op jit(solution)/shard_map/pallas_call | solution.py:200
  149.6 37.7 %all-gather.15.cloned.1.call-done = bf16[32,2,256,128]{3,2,1,0:T(8,128)(2,1)} async-done(((bf16[2,2,256,128]{3,2,1,0:T(8,128)(2,1)}), bf16[32,2,256,128]{3,2,1,0:T(8,128)(2,1)}) %all-gather.15.cloned.1.call-update) | async-done | bytes 4194320 | tf_op jit(solution)/shard_map/all_gather | solution.py:199
  187.3 2.2 copy-done.2
  189.5 1.6 copy-done.6
  191.1 16.1 %shard_map.49 = bf16[256,1024]{1,0:T(8,128)(2,1)S(1)} custom-call(s32[2]{0:T(128)S(1)} %get-tuple-element.14.me_ref, bf16[256,4096]{1,0:T(8,128)(2,1)S(1)} %copy-done.6, bf16[16,2,2,256,128]{4,3,2,1,0:T(8,128)(2,1)S(1)} %bitcast.26, bf16[256,128]{1,0:T(8,128)(2,1)S(1)} %pad.4.hide_ref, f32[8,256]{1,0:T(8,128)S(1)} %broadcast_in_dim.31.live_ref), custom_call_target="tpu_custom_call" | custom-call | flops 4294967296 | bytes 4194304 | tf_op jit(solution)/shard_map/pallas_call | solution.py:200
  207.2 37.4 %all-gather.13.cloned.1.call-done = bf16[32,2,256,128]{3,2,1,0:T(8,128)(2,1)} async-done(((bf16[2,2,256,128]{3,2,1,0:T(8,128)(2,1)}), bf16[32,2,256,128]{3,2,1,0:T(8,128)(2,1)}) %all-gather.13.cloned.1.call-update) | async-done | bytes 4194320 | tf_op jit(solution)/shard_map/all_gather | solution.py:199
  244.6 2.2 copy-done.3
  246.8 1.6 copy-done.7
  248.4 15.9 %shard_map.48 = bf16[256,1024]{1,0:T(8,128)(2,1)S(1)} custom-call(s32[2]{0:T(128)S(1)} %get-tuple-element.13.me_ref, bf16[256,4096]{1,0:T(8,128)(2,1)S(1)} %copy-done.7, bf16[16,2,2,256,128]{4,3,2,1,0:T(8,128)(2,1)S(1)} %bitcast.27, bf16[256,128]{1,0:T(8,128)(2,1)S(1)} %pad.4.hide_ref, f32[8,256]{1,0:T(8,128)S(1)} %broadcast_in_dim.31.live_ref), custom_call_target="tpu_custom_call" | custom-call | flops 4294967296 | bytes 4194304 | tf_op jit(solution)/shard_map/pallas_call | solution.py:200
  264.3 1.5 pad_maximum_fusion
  (29 shorter events, 1.1 us)
Async XLA Ops:
  6.5 65.9 %all-gather.9.cloned.1.call-start = ((), (), s32[]{:S(2)}) async-start(), calls=%async_computation | async-start | bytes 4456448 | tf_op jit(solution)/shard_map/all_gather | solution.py:199
  9.1 7.0 %copy-start.8 = (s32[32]{0:T(128)S(1)}, s32[32]{0:T(128)}, u32[]{:S(2)}) copy-start(s32[32]{0:T(128)} %param.6) | copy-start | bytes 388
  12.6 117.3 %all-gather.11.cloned.1.call-start = ((), (), s32[]{:S(2)}) async-start(), calls=%async_computation.1 | async-start | bytes 4456448 | tf_op jit(solution)/shard_map/all_gather | solution.py:199
  13.5 173.8 %all-gather.15.cloned.1.call-start = ((), (), s32[]{:S(2)}) async-start(), calls=%async_computation.3 | async-start | bytes 4456448 | tf_op jit(solution)/shard_map/all_gather | solution.py:199
  14.4 230.2 %all-gather.13.cloned.1.call-start = ((), (), s32[]{:S(2)}) async-start(), calls=%async_computation.2 | async-start | bytes 4456448 | tf_op jit(solution)/shard_map/all_gather | solution.py:199
  72.5 2.2 copy-start
  74.7 1.6 copy-start.4
  129.9 2.2 copy-start.1
  132.1 1.6 copy-start.5
  187.3 2.2 copy-start.2
  189.5 1.6 copy-start.6
  244.6 2.2 copy-start.3
  246.8 1.6 copy-start.7
Sparse Core Ops, SparseCore 0:
  12.7 59.7 all-gather.8
  74.9 54.9 all-gather.10
  132.4 54.9 all-gather.14
  189.6 54.9 all-gather.12

commit v2 on v0

v2 whole, which is shorter than its diff:
```python
import functools
import math

import jax
import jax.numpy as jnp
from jax import lax
from jax.experimental import pallas as pl
from jax.experimental.pallas import tpu as pltpu
from jax.sharding import PartitionSpec as P

KV_HEADS = 8
GROUP = 4
DIM = 128
SPAN = 128
BLOCKS = 16
PIECES = 4
PAIR = KV_HEADS // PIECES
RING = 4
EXP_SCALE = math.log2(math.e) / math.sqrt(DIM)
HIDDEN = -1e30
LIMIT = 2.0**110
SENDS = 60
NT = (((1,), (1,)), ((), ()))
MESH = pl.DeviceIdType.MESH


def scores_t(keys, queries):
    return lax.dot_general(keys, queries, NT, preferred_element_type=jnp.float32)


def weights_of(scores):
    return jnp.exp2(scores * EXP_SCALE).astype(jnp.bfloat16)


def with_ones(values_t):
    ones = jnp.ones((16, values_t.shape[1]), jnp.bfloat16)
    return jnp.concatenate([values_t, ones], axis=0)


def halves(block):
    return [block[t * SPAN : (t + 1) * SPAN] for t in range(block.shape[0] // SPAN)]


def gather_attend(
    q_hbm, own_hbm, hide_ref, *refs
):
    acc_refs, whole_hbm = refs[:GROUP], refs[GROUP]
    buf, q_ref, qx_ref, slot_ref, send_sem, recv_sem, own_sem, out_sem = refs[GROUP + 1 :]
    me = lax.axis_index("ctx")
    core = me % 2
    x = (me // 2) % RING
    y = me // (2 * RING)
    x_right, x_left, x_far = (x + 1) % RING, (x + 3) % RING, (x + 2) % RING
    y_far = 1 - y
    rows = q_ref.shape[0]
    spans = rows // SPAN

    def block_at(row, column):
        return (row * RING + column) * 2 + core

    right, left = block_at(y, x_right), block_at(y, x_left)
    partner, sibling = block_at(y_far, x), (y * RING + x) * 2 + 1 - core
    far = block_at(y, x_far)
    partner_left, partner_right = block_at(y_far, x_left), block_at(y_far, x_right)
    partner_far = block_at(y_far, x_far)

    barrier = pltpu.get_barrier_semaphore()
    for other in (right, left, partner, sibling):
        pl.semaphore_signal(barrier, inc=1, device_id={"ctx": other}, device_id_type=MESH)

    q_copy = pltpu.make_async_copy(q_hbm, q_ref, own_sem.at[0])
    own_copy = pltpu.make_async_copy(own_hbm, buf.at[me], own_sem.at[1])
    q_copy.start()
    own_copy.start()

    count = [0]

    def send(block, piece, target, source=None):
        pltpu.make_async_remote_copy(
            src_ref=buf.at[block, piece] if source is None else source,
            dst_ref=buf.at[block, piece],
            send_sem=send_sem.at[count[0]],
            recv_sem=recv_sem.at[block, piece],
            device_id={"ctx": target},
            device_id_type=MESH,
        ).start()
        count[0] += 1

    def arrived(block, piece):
        pltpu.make_async_remote_copy(
            src_ref=buf.at[block, piece],
            dst_ref=buf.at[block, piece],
            send_sem=send_sem.at[0],
            recv_sem=recv_sem.at[block, piece],
            device_id={"ctx": sibling},
            device_id_type=MESH,
        ).wait_recv()

    pl.semaphore_wait(barrier, 4)
    for j in range(PIECES):
        k = (j + 2) % PIECES
        send(me, j, right, own_hbm.at[j])
        send(me, k, left, own_hbm.at[k])
        send(me, k, partner, own_hbm.at[k])
        send(me, j, sibling, own_hbm.at[j])

    row = lax.broadcasted_iota(jnp.int32, (SPAN, SPAN), 0)
    lane = lax.broadcasted_iota(jnp.int32, (SPAN, SPAN), 1)
    for t in range(BLOCKS * spans):
        slot_ref[t] = jnp.where((lane == 0) | (lane == 1 + t), 1.0, 0.0).astype(jnp.bfloat16)
    q_copy.wait()
    own_copy.wait()

    @pl.loop(0, KV_HEADS)
    def _(g):
        piece, pair = g // PAIR, g % PAIR
        own_keys = buf[me, piece, 0, pair]
        own_values = halves(buf[me, piece, 1, pair])
        q_all = q_ref[:, pl.ds(pl.multiple_of(g * GROUP * DIM, GROUP * DIM), GROUP * DIM)]
        for i in range(GROUP):
            for t in range(spans):
                cut = slice(t * SPAN, (t + 1) * SPAN)
                q = q_all[cut, i * DIM : (i + 1) * DIM]
                keys = own_keys[cut]
                near = jnp.where(lane <= row, scores_t(q, keys), HIDDEN)
                best = jnp.max(near, axis=1, keepdims=True).astype(jnp.bfloat16)
                extra = jnp.where(
                    lane == 0, -best.astype(jnp.float32), hide_ref[cut].astype(jnp.float32)
                )
                q_x = jnp.concatenate([q, extra.astype(jnp.bfloat16)], axis=1)
                qx_ref[g, i, cut] = q_x
                first = jnp.where(lane == 0, 1.0, 0.0).astype(jnp.bfloat16)
                keys_x = jnp.concatenate([keys, first], axis=1)
                weights = weights_of(jnp.where(row <= lane, scores_t(keys_x, q_x), HIDDEN))
                acc_refs[i][g, :, cut] = jnp.dot(
                    with_ones(own_values[t]), weights, preferred_element_type=jnp.float32
                )

    def take(*pieces):
        for block, piece in pieces:
            arrived(block, piece)
            send(block, piece, sibling)

    def stage_0():
        take((left, 0), (right, 2), (partner, 2))
        send(left, 0, right)
        send(right, 2, left)
        take((left, 1), (right, 3), (partner, 3))
        send(left, 1, right)
        send(right, 3, left)
        for piece in (2, 3):
            send(partner, piece, right)
            send(partner, piece, left)

    def stage_1():
        take((left, 2), (right, 0), (partner, 0))
        send(partner, 0, right)
        send(partner, 0, left)

    def stage_2():
        take((left, 3), (right, 1), (partner, 1))
        send(partner, 1, right)
        send(partner, 1, left)

    def stage_3():
        for piece in (0, 2):
            take((far, piece))
            send(far, piece, partner)

    def stage_4():
        for piece in (1, 3):
            take((far, piece))
            send(far, piece, partner)
        take((partner_far, 0), (partner_left, 2), (partner_right, 2), (partner_far, 2))

    def stage_5():
        take((partner_left, 3), (partner_right, 3), (partner_far, 1))

    def stage_6():
        take((partner_left, 0), (partner_right, 0), (partner_far, 3))

    def stage_7():
        take((partner_left, 1), (partner_right, 1))

    stages = (stage_0, stage_1, stage_2, stage_3, stage_4, stage_5, stage_6, stage_7)

    def kept(block, piece, n):
        return pltpu.make_async_copy(buf.at[block, piece], whole_hbm.at[block, piece], out_sem.at[n])

    def pick(condition, a, b):
        return jnp.where(condition, a, b)

    def step(w, carry):
        for n, stage in enumerate(stages):
            pl.when(w == n)(stage)

        def tile(t, carry):
            late, second = w >= len(stages) // 2, t == 1
            turned = (w + 2) % PIECES
            swapped = (w % PIECES) // 2 + 2 * (w % 2)
            piece = pick(second, turned, pick(late, swapped, w % PIECES))
            one = pick(second, pick(late, partner_left, partner), pick(late, far, me))
            two = pick(second, pick(late, partner_right, right), pick(late, partner_far, left))
            other = 1 - 2 * core
            arrived(one + other, piece)
            arrived(two + other, piece)
            blocks = (one, one + other, two, two + other)
            for j, b in enumerate(blocks):
                kept(b, piece, (w * 2 + t) * 4 + j).start()

            def key_head(pair, carry):
                g = piece * PAIR + pair
                keys = jnp.concatenate([buf[b, piece, 0, pair] for b in blocks], axis=0)
                slots = jnp.concatenate(
                    [slot_ref[b * spans + s] for b in blocks for s in range(spans)], axis=0
                )
                keys_x = jnp.concatenate([keys, slots], axis=1)
                values_t = with_ones(
                    jnp.concatenate([v for b in blocks for v in halves(buf[b, piece, 1, pair])], axis=1)
                )

                def add(i, weights):
                    acc_refs[i][g] += jnp.dot(values_t, weights, preferred_element_type=jnp.float32)

                held = None
                for i in range(GROUP):
                    weights = weights_of(scores_t(keys_x, qx_ref[g, i]))
                    if held is not None:
                        add(i - 1, held)
                    held = weights
                add(GROUP - 1, held)
                return carry

            return lax.fori_loop(0, PAIR, key_head, carry)

        return lax.fori_loop(0, 2, tile, carry)

    lax.fori_loop(0, len(stages), step, 0)

    def drain(n, carry):
        pltpu.make_async_remote_copy(
            src_ref=buf.at[me, 0],
            dst_ref=buf.at[me, 0],
            send_sem=send_sem.at[n],
            recv_sem=recv_sem.at[me, 0],
            device_id={"ctx": sibling},
            device_id_type=MESH,
        ).wait_send()
        return carry

    assert count[0] == SENDS
    lax.fori_loop(0, SENDS, drain, 0)

    def drain_kept(n, carry):
        kept(me, 0, n).wait()
        return carry

    lax.fori_loop(0, BLOCKS * PIECES, drain_kept, 0)


def finish_attend(q_ref, hide_ref, live_ref, *refs):
    acc_in, (whole_hbm, o_ref, kv_ref, qx_ref, acc_ref, sem) = refs[:GROUP], refs[GROUP:]
    g = pl.program_id(0)
    me = lax.axis_index("ctx")
    rows = q_ref.shape[0]
    spans = rows // SPAN
    row = lax.broadcasted_iota(jnp.int32, (SPAN, SPAN), 0)
    lane = lax.broadcasted_iota(jnp.int32, (SPAN, SPAN), 1)
    live = live_ref[0:1]

    def finish(i, acc):
        out = jnp.where(live > 0.0, acc[:DIM] / acc[DIM : DIM + 1], 0.0)
        o_ref[:, i * DIM : (i + 1) * DIM] = out.T.astype(jnp.bfloat16)

    good = jnp.where(acc_in[0][0, DIM : DIM + 1] < LIMIT, 1.0, 0.0)
    for i in range(1, GROUP):
        good = jnp.where(acc_in[i][0, DIM : DIM + 1] < LIMIT, good, 0.0)
    for i in range(GROUP):
        finish(i, acc_in[i][0])

    @pl.when(jnp.min(good) < 0.5)
    def _():
        def fetch(b):
            copy = pltpu.make_async_copy(whole_hbm.at[b, g // PAIR, :, g % PAIR], kv_ref, sem)
            copy.start()
            copy.wait()

        for i in range(GROUP):
            fetch(me)
            parts = []
            for t in range(spans):
                cut = slice(t * SPAN, (t + 1) * SPAN)
                q = q_ref[cut, i * DIM : (i + 1) * DIM]
                near = jnp.where(row <= lane, scores_t(kv_ref[0, cut], q), HIDDEN)
                best = jnp.max(near, axis=0, keepdims=True)
                acc_ref[:, cut] = jnp.dot(
                    with_ones(kv_ref[1, cut]), weights_of(near - best), preferred_element_type=jnp.float32
                )
                extra = jnp.where(lane == 0, 0.0, hide_ref[cut].astype(jnp.float32))
                qx_ref[cut] = jnp.concatenate([q, extra.astype(jnp.bfloat16)], axis=1)
                parts.append(best)

            def absorb(b, best):
                fetch(b)
                key_row = lax.broadcasted_iota(jnp.int32, (rows, DIM), 0)
                slot = lax.broadcasted_iota(jnp.int32, (rows, DIM), 1) - 1 - b * spans
                slots = jnp.where(key_row // SPAN == slot, 1.0, 0.0).astype(jnp.bfloat16)
                scores = scores_t(jnp.concatenate([kv_ref[0], slots], axis=1), qx_ref[...])
                new = jnp.maximum(best, jnp.max(scores, axis=0, keepdims=True))
                values_t = with_ones(jnp.concatenate(halves(kv_ref[1]), axis=1))
                acc_ref[...] = acc_ref[...] * jnp.exp2((best - new) * EXP_SCALE) + jnp.dot(
                    values_t, weights_of(scores - new), preferred_element_type=jnp.float32
                )
                return new

            lax.fori_loop(0, BLOCKS, absorb, jnp.concatenate(parts, axis=1))
            finish(i, acc_ref[...])


def shards(queries, keys_values, fold, doc_length):
    me = lax.axis_index("ctx")
    rows = queries.shape[0]
    spans = rows // SPAN
    slots = fold.shape[0]

    split = keys_values.reshape(rows, 2, PIECES, PAIR, DIM)
    keys = split[:, 0].transpose(1, 2, 0, 3)
    values = split[:, 1].reshape(spans, SPAN, PIECES, PAIR, DIM).transpose(2, 3, 0, 4, 1)
    packed = jnp.stack([keys, values.reshape(PIECES, PAIR, rows, DIM)], axis=1)

    own = lax.dynamic_slice(fold, (me * spans,), (spans,))
    own_span = jnp.repeat(own, SPAN)
    hidden = fold[None, :] >= own_span[:, None]
    hide = jnp.where(hidden, HIDDEN, 0.0).astype(jnp.bfloat16)
    hide = jnp.pad(hide, ((0, 0), (1, DIM - 1 - slots)))
    position = own_span * SPAN + jnp.arange(rows, dtype=jnp.int32) % SPAN
    live = jnp.where(position < doc_length[0], 1.0, 0.0)
    live = jnp.broadcast_to(live[None, :], (8, rows))

    anywhere = pl.BlockSpec(memory_space=pl.ANY)
    in_vmem = pl.BlockSpec(memory_space=pltpu.VMEM)
    sums = jax.ShapeDtypeStruct((KV_HEADS, DIM + 16, rows), jnp.float32)
    whole = jax.ShapeDtypeStruct((BLOCKS, PIECES, 2, PAIR, rows, DIM), jnp.bfloat16)
    *accs, gathered = pl.pallas_call(
        gather_attend,
        in_specs=[anywhere, anywhere, in_vmem],
        out_specs=[in_vmem] * GROUP + [anywhere],
        out_shape=[sums] * GROUP + [whole],
        scratch_shapes=[
            pltpu.VMEM(whole.shape, jnp.bfloat16),
            pltpu.VMEM(queries.shape, jnp.bfloat16),
            pltpu.VMEM((KV_HEADS, GROUP, rows, 2 * DIM), jnp.bfloat16),
            pltpu.VMEM((slots, SPAN, DIM), jnp.bfloat16),
            pltpu.SemaphoreType.DMA((SENDS,)),
            pltpu.SemaphoreType.DMA((BLOCKS, PIECES)),
            pltpu.SemaphoreType.DMA((2,)),
            pltpu.SemaphoreType.DMA((BLOCKS * PIECES,)),
        ],
        compiler_params=pltpu.CompilerParams(
            collective_id=0, has_side_effects=True, vmem_limit_bytes=48 * 2**20
        ),
    )(queries, packed, hide)

    return pl.pallas_call(
        finish_attend,
        grid=(KV_HEADS,),
        in_specs=[
            pl.BlockSpec((rows, GROUP * DIM), lambda g: (0, g)),
            pl.BlockSpec((rows, DIM), lambda g: (0, 0)),
            pl.BlockSpec((8, rows), lambda g: (0, 0)),
        ]
        + [pl.BlockSpec((1, DIM + 16, rows), lambda g: (g, 0, 0))] * GROUP
        + [anywhere],
        out_specs=pl.BlockSpec((rows, GROUP * DIM), lambda g: (0, g)),
        out_shape=jax.ShapeDtypeStruct(queries.shape, jnp.bfloat16),
        scratch_shapes=[
            pltpu.VMEM((2, rows, DIM), jnp.bfloat16),
            pltpu.VMEM((rows, 2 * DIM), jnp.bfloat16),
            pltpu.VMEM((DIM + 16, rows), jnp.float32),
            pltpu.SemaphoreType.DMA,
        ],
        compiler_params=pltpu.CompilerParams(vmem_limit_bytes=24 * 2**20),
    )(queries, hide, live, *accs, gathered)


def solution(mesh):
    in_specs = (P(("dp", "ctx"), None), P(("dp", "ctx"), None, None), P("dp"), P("dp"))
    out_specs = P(("dp", "ctx"), None)
    return jax.shard_map(shards, mesh=mesh, in_specs=in_specs, out_specs=out_specs, check_vma=False)
```

time: 453 us -> 93.9 us (0.21)
  the two profiles are of different devices: /device:TPU:80 before, /device:TPU:1 now
where the time goes in v2:
time: 93.9 us; the launch traced here: 93.7 us
  Pallas kernels  82.3 us (88%)
  local copies, waits for them, and re-layouts  9.67 us (10%)
    pallas_call x1, Pallas kernels, shards(): pl.pallas_call(gather_attend, in_specs=[anywhere, anywhere, in_vmem], out...  78.5 us
    unnamed x6, local copies, waits for them, and re-layouts  8.46 us
    pallas_call x1, Pallas kernels, shards(): pl.pallas_call(finish_attend, grid=(KV_HEADS,), in_specs=[pl.BlockSpec((r...  3.83 us

profile of v2, /device:TPU:1, one launch (start us, length us, event | category | flops | bytes accessed | tf_op | source)
XLA Modules:
  0.0 93.7 jit_solution(14854144190275998926)
XLA Ops:
  0.7 0.7 dynamic_slice.3
  1.4 0.1 compare_select_fusion
  1.5 0.1 broadcast_bitcast_fusion
  1.5 0.8 select_convert_fusion
  2.3 0.1 pad.4.hide_ref
  2.4 2.4 %copy.6 = bf16[256,2,1024]{0,2,1:T(8,128)(2,1)S(1)} copy(bf16[256,2,1024]{2,1,0:T(2,128)(2,1)} %param.5) | data formatting | bytes 2097152 | tf_op args[1]
  4.8 0.1 fusion.1
  4.9 0.3 copy.9
  5.2 0.1 reshape_squeeze.3
  5.3 0.1 copy.8
  5.4 0.1 pad_maximum_fusion.own_hbm
  5.5 0.0 copy-start.1
  5.6 78.5 %shard_map.46 = (f32[8,144,256]{2,1,0:T(8,128)S(1)}, f32[8,144,256]{2,1,0:T(8,128)S(1)}, f32[8,144,256]{2,1,0:T(8,128)S(1)}, f32[8,144,256]{2,1,0:T(8,128)S(1)}, bf16[16,4,2,2,256,128]{5,4,3,2,1,0:T(8,128)(2,1)}) custom-call(bf16[256,4096]{1,0:T(8,128)(2,1)} %q_ref.1, bf16[4,2,2,256,128]{4,3,2,1,0:T(8,128)(2,1)S(1)} %pad_maximum_fusion.own_hbm, ...), custom_call_target="tpu_custom_call" | custom-call | tf_op jit(solution)/shard_map/pallas_call | solution.py:344
  84.1 0.0 copy-done.1
  84.1 0.0 copy-start
  84.1 5.8 %copy-done = bf16[16,4,2,2,256,128]{5,4,3,2,1,0:T(8,128)(2,1)S(1)} copy-done((bf16[16,4,2,2,256,128]{5,4,3,2,1,0:T(8,128)(2,1)S(1)}, bf16[16,4,2,2,256,128]{5,4,3,2,1,0:T(8,128)(2,1)}, u32[]{:S(2)}) %copy-start) | copy-done | bytes 16777240
  89.8 3.8 %shard_map.47 = bf16[256,4096]{1,0:T(8,128)(2,1)} custom-call(bf16[256,4096]{1,0:T(8,128)(2,1)S(1)} %copy-done.1, bf16[256,128]{1,0:T(8,128)(2,1)S(1)} %pad.4.hide_ref, f32[8,256]{1,0:T(8,128)S(1)} %broadcast_in_dim.31.live_ref, f32[8,144,256]{2,1,0:T(8,128)S(1)} %get-tuple-element.10.refs_0_, f32[8,144,256]{2,1,0:T(8,128)S(1)} %get-tuple-element.11.refs_1_, ...), custom_call_target="tpu_custom_call" | custom-call | tf_op jit(solution)/shard_map/pallas_call | solution.py:364
  (1 shorter events, 0.0 us)
Async XLA Ops:
  5.5 78.5 %copy-start.1 = (bf16[256,4096]{1,0:T(8,128)(2,1)S(1)}, bf16[256,4096]{1,0:T(8,128)(2,1)}, u32[]{:S(2)}) copy-start(bf16[256,4096]{1,0:T(8,128)(2,1)} %q_ref.1) | copy-start | bytes 6291460
  84.1 5.8 %copy-start = (bf16[16,4,2,2,256,128]{5,4,3,2,1,0:T(8,128)(2,1)S(1)}, bf16[16,4,2,2,256,128]{5,4,3,2,1,0:T(8,128)(2,1)}, u32[]{:S(2)}) copy-start(bf16[16,4,2,2,256,128]{5,4,3,2,1,0:T(8,128)(2,1)} %get-tuple-element.14.refs_4_) | copy-start | bytes 50331652
